TPU v7x, 32 devices: a whole 2x2x4 slice. The times are simulated.
32 devices in a mesh: replica: 8 (over z, core), shard: 4 (over y, x).
Axes of the slice: x: 2, y: 2, z: 4, core: 2. Of those that a mesh axis runs over, the one named last changes fastest.
Arguments:
- hidden_in: bfloat16 [4, 2048, 2048], P('shard', 'replica'), may hold values from -6 to 6
- piece_index: int32 [4, 2048], P('shard', 'replica'), may hold values from -1 to 7, as said below
- pad_flags: int32 [4, 2048], P('shard', 'replica'), may hold values from 0 to 1, as said below
- cotangent: bfloat16 [4, 2048, 2048], P('shard', 'replica'), may hold values from -6 to 6
- query_weight: bfloat16 [2048, 2048], P('shard'), may hold values from -0.125 to 0.125
- key_weight: bfloat16 [2048, 2048], P('shard'), may hold values from -0.125 to 0.125
- value_weight: bfloat16 [2048, 2048], P('shard'), may hold values from -0.125 to 0.125
- output_weight: bfloat16 [2048, 2048], P('shard'), may hold values from -0.125 to 0.125
- gate_weight: bfloat16 [2048, 8192], P('shard'), may hold values from -0.125 to 0.125
- up_weight: bfloat16 [2048, 8192], P('shard'), may hold values from -0.125 to 0.125
- down_weight: bfloat16 [8192, 2048], P('shard'), may hold values from -0.0625 to 0.0625
- query_gain: bfloat16 [2048], P('shard'), may hold values from 0.25 to 1.75
- key_gain: bfloat16 [2048], P('shard'), may hold values from 0.25 to 1.75
- attention_gain: bfloat16 [2048], P('shard'), may hold values from 0.25 to 1.75
- feed_gain: bfloat16 [2048], P('shard'), may hold values from 0.25 to 1.75
Outputs:
- result: float32 [4, 2048, 2048], P('shard', 'replica')
- grad_hidden: float32 [4, 2048, 2048], P('shard', 'replica')
- grad_query_weight: float32 [2048, 2048], P('shard')
- grad_key_weight: float32 [2048, 2048], P('shard')
- grad_value_weight: float32 [2048, 2048], P('shard')
- grad_output_weight: float32 [2048, 2048], P('shard')
- grad_gate_weight: float32 [2048, 8192], P('shard')
- grad_up_weight: float32 [2048, 8192], P('shard')
- grad_down_weight: float32 [8192, 2048], P('shard')
- grad_query_gain: float32 [2048], P('shard')
- grad_key_gain: float32 [2048], P('shard')
- grad_attention_gain: float32 [2048], P('shard')
- grad_feed_gain: float32 [2048], P('shard')
- stats: float32 [3], replicated
Inputs may be any that keep to these rules, and one draw needn't show every extreme that they name: `piece_index`: -1 marks text. A picture piece is an aligned run of 256 tokens of one sequence, all holding that run's index within the sequence; the first run of every sequence is text and the last run of every sequence is a picture piece. `pad_flags`: each sequence ends in a run of one or more padded tokens and has none elsewhere.
All inputs are finite; a program needn't handle non-finite values.
Results may differ from a plain program's by a relative error of at most 0.025.
Values may be sent and summed in bfloat16 or wider, within the bound.
No kernel may reach another device: no remote copies, remote signals or barrier semaphores. Data moves between devices by JAX's collectives and lax.ppermute only.
A program may use at most 576 MiB of HBM per device.

v0:
```python
import math
import jax
import jax.numpy as jnp
from jax import lax
from jax.sharding import PartitionSpec as P

HEADS = 16
HEAD = 128
epsilon = 1e-06
theta_base = 500000.0
masked_score = -1e30


def norm_rows(values, gain):
    scaled = values * lax.rsqrt(jnp.mean(values * values, axis=-1, keepdims=True) + epsilon)
    return scaled * gain


def angle_table(positions):
    half_head = HEAD // 2
    rates = theta_base ** (-jnp.arange(half_head).astype(jnp.float32) * (2.0 / HEAD))
    angles = positions.astype(jnp.float32)[:, None] * rates[None, :]
    return (jnp.cos(angles), jnp.sin(angles))


def rotate(values, cosine, sine):
    half_head = HEAD // 2
    first_half = values[..., :half_head]
    second_half = values[..., half_head:]
    cos_wide = cosine[:, None, :]
    sin_wide = sine[:, None, :]
    return jnp.concatenate(
        [
            first_half * cos_wide - second_half * sin_wide,
            second_half * cos_wide + first_half * sin_wide,
        ],
        axis=-1,
    )


def turn_heads(flat_rows, gain, cosine, sine):
    rows_here = flat_rows.shape[0]
    normed = norm_rows(flat_rows, gain).reshape(rows_here, HEADS, HEAD)
    return rotate(normed, cosine, sine).reshape(rows_here, HEADS * HEAD)


def contract_rows(left, right):
    return lax.dot_general(
        left, right, (((0,), (0,)), ((), ())), preferred_element_type=jnp.float32
    )


def contract_cols(left, right):
    return lax.dot_general(
        left, right, (((1,), (1,)), ((), ())), preferred_element_type=jnp.float32
    )


def block_scores(queries, keys_part, info_part, query_place, query_piece, start_key):
    rows_here = queries.shape[0]
    block_rows = keys_part.shape[0]
    scores = jnp.einsum(
        "qhd,khd->hqk",
        queries.reshape(rows_here, HEADS, HEAD),
        keys_part.reshape(block_rows, HEADS, HEAD),
        preferred_element_type=jnp.float32,
    ) * HEAD ** (-0.5)
    key_place = start_key + jnp.arange(block_rows, dtype=jnp.int32)
    key_piece = info_part.astype(jnp.float32)
    allowed = (key_place[None, :] <= query_place[:, None]) | (query_piece[:, None] >= 0.0) & (
        query_piece[:, None] == key_piece[None, :]
    )
    allowed = allowed & (key_piece[None, :] > -1.5)
    return jnp.where(allowed[None], scores, masked_score)


def per_device(
    hidden_in,
    piece_index,
    pad_flags,
    cotangent,
    query_weight,
    key_weight,
    value_weight,
    output_weight,
    gate_weight,
    up_weight,
    down_weight,
    query_gain,
    key_gain,
    attention_gain,
    feed_gain,
):
    tokens = hidden_in[0]
    rows_here = tokens.shape[0]
    width_all = tokens.shape[1]
    hidden_all = gate_weight.shape[1]
    seq_len = rows_here * lax.axis_size("replica")
    first_row = lax.axis_index("replica") * rows_here
    positions = first_row + jnp.arange(rows_here, dtype=jnp.int32)
    cosine, sine = angle_table(positions)
    score_scale = HEAD ** (-0.5)
    input_whole = ()
    feed_whole = ()
    start = jnp.int32(0)
    whole_in = input_whole
    piece_query = lax.all_gather(query_weight, "shard", axis=0, tiled=True)
    piece_key = lax.all_gather(key_weight, "shard", axis=0, tiled=True)
    piece_value = lax.all_gather(value_weight, "shard", axis=0, tiled=True)
    piece_out = lax.all_gather(output_weight, "shard", axis=0, tiled=True)
    gain_one = lax.all_gather(query_gain, "shard", axis=0, tiled=True)
    gain_two = lax.all_gather(key_gain, "shard", axis=0, tiled=True)
    gain_three = lax.all_gather(attention_gain, "shard", axis=0, tiled=True)
    gain_four = lax.all_gather(feed_gain, "shard", axis=0, tiled=True)
    columns = tokens
    sums = tuple(
        (
            jnp.dot(columns, piece, preferred_element_type=jnp.float32)
            for piece in (piece_query, piece_key, piece_value)
        )
    )
    stacked = jnp.stack([gain_one, gain_two, gain_three, gain_four])
    gain_rows = stacked
    whole_in = tuple(
        (
            lax.dynamic_update_slice_in_dim(whole, piece, start, 0)
            for whole, piece in zip(whole_in, (piece_query, piece_key, piece_value))
        )
    )
    (query_raw, key_raw, value_raw), out_whole, gain_rows, input_whole = (
        sums,
        piece_out,
        gain_rows,
        whole_in,
    )
    gains_wide = gain_rows.astype(jnp.float32)

    def turn_local(raw_rows, gain):
        return turn_heads(raw_rows, gain, cosine, sine)

    query_turned, query_pull = jax.vjp(turn_local, query_raw, gains_wide[0])
    key_turned, key_pull = jax.vjp(turn_local, key_raw, gains_wide[1])
    query_low = query_turned.astype(jnp.bfloat16)
    key_low = key_turned.astype(jnp.bfloat16)
    value_low = value_raw.astype(jnp.bfloat16)
    key_info = jnp.where(pad_flags[0] > 0, -2, piece_index[0]).astype(jnp.bfloat16)
    keys_all, values_all, info_all = (
        lax.all_gather(key_low, "replica", axis=0, tiled=True),
        lax.all_gather(value_low, "replica", axis=0, tiled=True),
        lax.all_gather(key_info, "replica", axis=0, tiled=True),
    )
    query_piece = piece_index[0].astype(jnp.float32)
    block_rows = math.gcd(seq_len, 512)
    block_count = seq_len // block_rows

    def scores_at(index):
        start_key = index * block_rows
        keys_part = lax.dynamic_slice_in_dim(keys_all, start_key, block_rows, 0)
        info_part = lax.dynamic_slice_in_dim(info_all, start_key, block_rows, 0)
        return block_scores(query_low, keys_part, info_part, positions, query_piece, start_key)

    def bound_step(index, carried):
        highest, summed = carried
        scores = scores_at(index)
        raised = jnp.maximum(highest, jnp.max(scores, axis=-1))
        summed = summed * jnp.exp(highest - raised) + jnp.sum(
            jnp.exp(scores - raised[..., None]), axis=-1
        )
        return (raised, summed)

    highest, summed = lax.fori_loop(
        0,
        block_count,
        bound_step,
        (
            jnp.full((HEADS, rows_here), masked_score, jnp.float32),
            jnp.zeros((HEADS, rows_here), jnp.float32),
        ),
    )
    log_total = highest + jnp.log(summed)

    def value_step(index, carried):
        start_key = index * block_rows
        weights_low = jnp.exp(scores_at(index) - log_total[..., None]).astype(jnp.bfloat16)
        values_part = lax.dynamic_slice_in_dim(values_all, start_key, block_rows, 0).reshape(
            block_rows, HEADS, HEAD
        )
        return carried + jnp.einsum(
            "hqk,khd->qhd", weights_low, values_part, preferred_element_type=jnp.float32
        )

    mixed = lax.fori_loop(
        0, block_count, value_step, jnp.zeros((rows_here, HEADS, HEAD), jnp.float32)
    )
    attended_low = mixed.reshape(rows_here, width_all).astype(jnp.bfloat16)
    branch_attn = jnp.dot(attended_low, out_whole, preferred_element_type=jnp.float32)
    normed_attn, attn_pull = jax.vjp(norm_rows, branch_attn, gains_wide[2])
    residual = tokens.astype(jnp.float32) + normed_attn
    residual_low = residual.astype(jnp.bfloat16)
    pieces = (
        lax.all_gather(gate_weight, "shard", axis=0, tiled=True),
        lax.all_gather(up_weight, "shard", axis=0, tiled=True),
    )
    start = jnp.int32(0)
    whole_list = feed_whole
    columns = residual_low
    sums = tuple((jnp.dot(columns, piece, preferred_element_type=jnp.float32) for piece in pieces))
    whole_list = tuple(
        (
            lax.dynamic_update_slice_in_dim(whole, piece, start, 0)
            for whole, piece in zip(whole_list, pieces)
        )
    )
    (gate_sum, up_sum), feed_whole = (sums, whole_list)

    def activate(gate_values, up_values):
        return jax.nn.silu(gate_values) * up_values

    activated, act_pull = jax.vjp(activate, gate_sum, up_sum)
    activated_low = activated.astype(jnp.bfloat16)
    piece = lax.all_gather(down_weight, "shard", axis=0, tiled=True)
    columns = activated_low
    partial_sum = jnp.dot(columns, piece, preferred_element_type=jnp.float32)
    normed_feed, feed_pull = jax.vjp(norm_rows, partial_sum, gains_wide[3])
    result = residual + normed_feed
    grad_out = cotangent[0].astype(jnp.float32)
    grad_feed, grad_feed_gain = feed_pull(grad_out)
    grad_feed_low = grad_feed.astype(jnp.bfloat16)
    grad_act = contract_cols(
        grad_feed_low, lax.all_gather(down_weight, "shard", axis=0, tiled=True)
    )
    down_share = lax.psum_scatter(
        contract_rows(activated_low, grad_feed_low).astype(jnp.bfloat16),
        "shard",
        scatter_dimension=0,
        tiled=True,
    ).astype(jnp.float32)
    grad_gate, grad_up = act_pull(grad_act)
    grad_gate_low = grad_gate.astype(jnp.bfloat16)
    grad_up_low = grad_up.astype(jnp.bfloat16)
    pieces = (
        lax.all_gather(gate_weight, "shard", axis=0, tiled=True),
        lax.all_gather(up_weight, "shard", axis=0, tiled=True),
    )
    part_sum = contract_cols(grad_gate_low, pieces[0]) + contract_cols(grad_up_low, pieces[1])
    grad_feed_in = part_sum
    grad_both = jnp.concatenate([grad_gate_low, grad_up_low], axis=1)
    feed_share = lax.psum_scatter(
        contract_rows(residual_low, grad_both).astype(jnp.bfloat16),
        "shard",
        scatter_dimension=0,
        tiled=True,
    ).astype(jnp.float32)
    grad_resid = grad_out + grad_feed_in
    grad_branch, grad_attention_gain = attn_pull(grad_resid)
    grad_branch_low = grad_branch.astype(jnp.bfloat16)
    grad_attended = contract_cols(
        grad_branch_low, lax.all_gather(output_weight, "shard", axis=0, tiled=True)
    )
    grad_mixed = grad_attended.astype(jnp.bfloat16).reshape(rows_here, HEADS, HEAD)
    delta = jnp.einsum("qhd,qhd->hq", grad_mixed.astype(jnp.float32), mixed)
    query_heads = query_low.reshape(rows_here, HEADS, HEAD)

    def back_step(index, carried):
        grad_query, grad_keys, grad_values = carried
        start_key = index * block_rows
        probs = jnp.exp(scores_at(index) - log_total[..., None])
        keys_part = lax.dynamic_slice_in_dim(keys_all, start_key, block_rows, 0).reshape(
            block_rows, HEADS, HEAD
        )
        values_part = lax.dynamic_slice_in_dim(values_all, start_key, block_rows, 0).reshape(
            block_rows, HEADS, HEAD
        )
        value_share = jnp.einsum(
            "hqk,qhd->khd",
            probs.astype(jnp.bfloat16),
            grad_mixed,
            preferred_element_type=jnp.float32,
        )
        grad_probs = jnp.einsum(
            "qhd,khd->hqk", grad_mixed, values_part, preferred_element_type=jnp.float32
        )
        grad_scores = (probs * (grad_probs - delta[..., None])).astype(jnp.bfloat16)
        grad_query = grad_query + jnp.einsum(
            "hqk,khd->qhd", grad_scores, keys_part, preferred_element_type=jnp.float32
        )
        key_share = (
            jnp.einsum("hqk,qhd->khd", grad_scores, query_heads, preferred_element_type=jnp.float32)
            * score_scale
        )
        grad_keys = lax.dynamic_update_slice_in_dim(
            grad_keys, key_share.reshape(block_rows, width_all), start_key, 0
        )
        grad_values = lax.dynamic_update_slice_in_dim(
            grad_values, value_share.reshape(block_rows, width_all), start_key, 0
        )
        return (grad_query, grad_keys, grad_values)

    zero_keys = jnp.zeros((seq_len, width_all), jnp.float32)
    grad_query, grad_keys, grad_values = lax.fori_loop(
        0,
        block_count,
        back_step,
        (jnp.zeros((rows_here, HEADS, HEAD), jnp.float32), zero_keys, zero_keys),
    )
    key_sum, value_sum = (
        lax.psum_scatter(
            grad_keys.astype(jnp.bfloat16), "replica", scatter_dimension=0, tiled=True
        ).astype(jnp.float32),
        lax.psum_scatter(
            grad_values.astype(jnp.bfloat16), "replica", scatter_dimension=0, tiled=True
        ).astype(jnp.float32),
    )
    grad_query_raw, grad_query_gain = query_pull(
        (grad_query * score_scale).reshape(rows_here, width_all)
    )
    grad_key_raw, grad_key_gain = key_pull(key_sum)
    query_back_low = grad_query_raw.astype(jnp.bfloat16)
    key_back_low = grad_key_raw.astype(jnp.bfloat16)
    value_back_low = value_sum.astype(jnp.bfloat16)
    pieces = (
        lax.all_gather(query_weight, "shard", axis=0, tiled=True),
        lax.all_gather(key_weight, "shard", axis=0, tiled=True),
        lax.all_gather(value_weight, "shard", axis=0, tiled=True),
    )
    part_sum = (
        contract_cols(query_back_low, pieces[0])
        + contract_cols(key_back_low, pieces[1])
        + contract_cols(value_back_low, pieces[2])
    )
    grad_tokens = grad_resid + part_sum
    grad_inputs = jnp.concatenate([query_back_low, key_back_low, value_back_low], axis=1)
    input_share = lax.psum_scatter(
        jnp.concatenate(
            [contract_rows(tokens, grad_inputs), contract_rows(attended_low, grad_branch_low)],
            axis=1,
        ).astype(jnp.bfloat16),
        "shard",
        scatter_dimension=0,
        tiled=True,
    ).astype(jnp.float32)
    input_share, feed_share, down_share = (
        lax.psum(input_share.astype(jnp.bfloat16), "replica").astype(jnp.float32),
        lax.psum(feed_share.astype(jnp.bfloat16), "replica").astype(jnp.float32),
        lax.psum(down_share.astype(jnp.bfloat16), "replica").astype(jnp.float32),
    )
    valid = (pad_flags[0] == 0).astype(jnp.float32)[:, None]
    stat_terms = jnp.stack(
        [
            jnp.sum(valid * result * result),
            jnp.sum(valid * branch_attn * branch_attn),
            jnp.sum(valid * partial_sum * partial_sum),
            jnp.sum(valid),
        ]
    )
    gain_terms = jnp.stack([grad_query_gain, grad_key_gain, grad_attention_gain, grad_feed_gain])
    gain_terms, stat_terms = lax.psum((gain_terms, stat_terms), ("replica", "shard"))
    gain_width = query_gain.shape[0]
    gain_mine = lax.dynamic_slice_in_dim(
        gain_terms, lax.axis_index("shard") * gain_width, gain_width, 1
    )
    stats = jnp.sqrt(stat_terms[:3] / (stat_terms[3] * width_all))
    return (
        result[None],
        grad_tokens[None],
        input_share[:, :width_all],
        input_share[:, width_all : 2 * width_all],
        input_share[:, 2 * width_all : 3 * width_all],
        input_share[:, 3 * width_all :],
        feed_share[:, :hidden_all],
        feed_share[:, hidden_all:],
        down_share,
        gain_mine[0],
        gain_mine[1],
        gain_mine[2],
        gain_mine[3],
        stats,
    )


def solution(mesh):
    placed = (
        P("shard", "replica", None),
        P("shard", "replica"),
        P("shard", "replica"),
        P("shard", "replica", None),
        P("shard", None),
        P("shard", None),
        P("shard", None),
        P("shard", None),
        P("shard", None),
        P("shard", None),
        P("shard", None),
        P("shard"),
        P("shard"),
        P("shard"),
        P("shard"),
    )
    return jax.shard_map(
        per_device,
        mesh=mesh,
        in_specs=placed,
        out_specs=(
            P("shard", "replica", None),
            P("shard", "replica", None),
            P("shard", None),
            P("shard", None),
            P("shard", None),
            P("shard", None),
            P("shard", None),
            P("shard", None),
            P("shard", None),
            P("shard"),
            P("shard"),
            P("shard"),
            P("shard"),
            P(),
        ),
        check_vma=False,
    )
```

profile of v0, /device:TPU:0, one launch (start us, length us, event | category | flops | bytes accessed | tf_op | source)
XLA Modules:
  0.0 3683.2 jit_solution(10131605898892978450)
XLA Ops:
  9.5 90.7 %all-gather.15.cloned.1.call-done = bf16[2048,2048]{1,0:T(8,128)(2,1)} async-done(((bf16[512,2048]{1,0:T(8,128)(2,1)}), bf16[2048,2048]{1,0:T(8,128)(2,1)}) %all-gather.15.cloned.1.call-update) | async-done | bytes 8388624 | tf_op jit(solution)/shard_map/all_gather | solution.py:109
  138.4 51.5 %all-gather.19.cloned.1.call-done = bf16[2048,2048]{1,0:T(8,128)(2,1)} async-done(((bf16[512,2048]{1,0:T(8,128)(2,1)}), bf16[2048,2048]{1,0:T(8,128)(2,1)}) %all-gather.19.cloned.1.call-update) | async-done | bytes 8388624 | tf_op jit(solution)/shard_map/all_gather | solution.py:108
  217.7 61.7 %all-gather.23.cloned.1.call-done = bf16[2048,2048]{1,0:T(8,128)(2,1)} async-done(((bf16[512,2048]{1,0:T(8,128)(2,1)}), bf16[2048,2048]{1,0:T(8,128)(2,1)}) %all-gather.23.cloned.1.call-update) | async-done | bytes 8388624 | tf_op jit(solution)/shard_map/all_gather | solution.py:107
  291.6 71.9 %all-gather.17.cloned.1.call-done = bf16[2048,2048]{1,0:T(8,128)(2,1)} async-done(((bf16[256,2048]{1,0:T(8,128)(2,1)}), bf16[2048,2048]{1,0:T(8,128)(2,1)}) %all-gather.17.cloned.1.call-update) | async-done | bytes 8388624 | tf_op jit(solution)/shard_map/all_gather | solution.py:149
  375.9 70.7 %all-gather.21.cloned.1.call-done = bf16[2048,2048]{0,1:T(8,128)(2,1)} async-done(((bf16[256,2048]{0,1:T(8,128)(2,1)}), bf16[2048,2048]{0,1:T(8,128)(2,1)}) %all-gather.21.cloned.1.call-update) | async-done | bytes 8388624 | tf_op jit(solution)/shard_map/all_gather | solution.py:148
  446.6 51.6 %while.48 = (s32[]{:T(128)}, f32[16,256]{1,0:T(8,128)S(1)}, f32[16,256]{1,0:T(8,128)S(1)}, f32[256]{0:T(256)S(1)}, bf16[2048]{0:T(1024)(128)(2,1)S(1)}, /*index=...) while((s32[]{:T(128)}, f32[16,256]{1,0:T(8,128)S(1)}, ...), condition=%wide.region_5.6_spmd.clone, body=%wide.region_2.5_spmd.clone.sunk | while | flops 552229376 | bytes 24739520 | solution.py:171
  498.2 42.5 %while.49 = (s32[]{:T(128)}, f32[256,16,128]{0,2,1:T(8,128)}, bf16[2048,2048]{0,1:T(8,128)(2,1)}, f32[256]{0:T(256)S(1)}, bf16[2048]{0:T(1024)(128)(2,1)S(1)}, /...) while((s32[]{:T(128)}, f32[256,16,128]{0,2,1:T(8,128)}, ...), condition=%wide.region_7.8_spmd.clone, body=%wide.region_6.7_spmd.clone.sunk | while | flops 1083836928 | bytes 18120392 | solution.py:192
  554.1 279.1 %all-gather.27.cloned.1.call-done = bf16[2048,8192]{1,0:T(8,128)(2,1)} async-done(((bf16[512,8192]{1,0:T(8,128)(2,1)}), bf16[2048,8192]{1,0:T(8,128)(2,1)}) %all-gather.27.cloned.1.call-update) | async-done | bytes 33554448 | tf_op jit(solution)/shard_map/all_gather | solution.py:201
  833.2 22.2 fusion.92
  855.5 276.8 %all-gather.29.cloned.1.call-done = bf16[2048,8192]{1,0:T(8,128)(2,1)} async-done(((bf16[512,8192]{1,0:T(8,128)(2,1)}), bf16[2048,8192]{1,0:T(8,128)(2,1)}) %all-gather.29.cloned.1.call-update) | async-done | bytes 33554448 | tf_op jit(solution)/shard_map/all_gather | solution.py:202
  1132.3 26.9 multiply_convert_fusion.1
  1159.2 272.2 %all-gather.31.cloned.1.call-done = bf16[8192,2048]{1,0:T(8,128)(2,1)} async-done(((bf16[2048,2048]{1,0:T(8,128)(2,1)}), bf16[8192,2048]{1,0:T(8,128)(2,1)}) %all-gather.31.cloned.1.call-update) | async-done | bytes 33554448 | tf_op jit(solution)/shard_map/all_gather | solution.py:221
  1450.1 22.0 multiply_convert_fusion
  1489.2 20.5 multiply_reduce_fusion.1
  1531.4 106.4 %while.50 = (s32[]{:T(128)}, f32[256,16,128]{0,2,1:T(8,128)}, bf16[2048,2048]{0,1:T(8,128)(2,1)}, bf16[2048,2048]{1,0:T(8,128)(2,1)}, bf16[2048,2048]{0,1:T(8,12...) while((s32[]{:T(128)}, f32[256,16,128]{0,2,1:T(8,128)}, ...), condition=%wide.region_13.14_spmd.clone, body=%wide.region_12.13_spmd.clone.sunk | while | flops 2709129728 | bytes 103219016 | solution.py:300
  1665.9 61.8 %reduce-scatter.10.cloned.1.call-done = bf16[256,2048]{0,1:T(8,128)(2,1)} async-done(((bf16[2048,2048]{0,1:T(8,128)(2,1)}), bf16[256,2048]{0,1:T(8,128)(2,1)}) %reduce-scatter.10.cloned.1.call-update) | async-done | bytes 1048592 | tf_op jit(solution)/shard_map/reduce_scatter | solution.py:307
  1741.6 76.9 %reduce-scatter.12.cloned.1.call-done = bf16[256,2048]{1,0:T(8,128)(2,1)} async-done(((bf16[2048,2048]{1,0:T(8,128)(2,1)}), bf16[256,2048]{1,0:T(8,128)(2,1)}) %reduce-scatter.12.cloned.1.call-update) | async-done | bytes 1048592 | tf_op jit(solution)/shard_map/reduce_scatter | solution.py:310
  1831.8 24.4 pad_maximum_fusion
  1857.4 29.1 convolution_convert_fusion
  1886.8 221.6 %reduce-scatter.18.cloned.1.call-done = bf16[2048,2048]{1,0:T(8,128)(2,1)} async-done(((bf16[8192,2048]{1,0:T(8,128)(2,1)}), bf16[2048,2048]{1,0:T(8,128)(2,1)}) %reduce-scatter.18.cloned.1.call-update) | async-done | bytes 8388624
  2108.4 292.0 %reduce-scatter.14.cloned.1.call-done = bf16[512,8192]{0,1:T(8,128)(2,1)} async-done(((bf16[2048,8192]{0,1:T(8,128)(2,1)}), bf16[512,8192]{0,1:T(8,128)(2,1)}) %reduce-scatter.14.cloned.1.call-update) | async-done | bytes 8388624 | tf_op jit(solution)/shard_map/reduce_scatter | solution.py:333
  2400.5 561.2 %reduce-scatter.16.cloned.1.call-done = bf16[512,16384]{1,0:T(8,128)(2,1)} async-done(((bf16[2048,16384]{1,0:T(8,128)(2,1)}), bf16[512,16384]{1,0:T(8,128)(2,1)}) %reduce-scatter.16.cloned.1.call-update) | async-done | bytes 16777232
  2965.6 41.1 %all-reduce.6 = (f32[4,2048]{1,0:T(4,128)S(1)}, f32[4]{0:T(128)S(1)}) all-reduce(f32[4,2048]{1,0:T(4,128)S(1)} %pad_maximum_fusion.2, f32[4]{0:T(128)S(1)} %pad_maximum_fusion.3), channel_id=1, replica_groups=mesh['replica'=8,'shard'=4] {'replica','shard'}, use_global_device_ids=true, to_apply=%region_28.29 | all-reduce | flops 8196 | bytes 65568 | tf_op jit(solution)/shard_map/psum | solution.py:357
  3025.0 591.2 %all-reduce.10.cloned.1.call-done = (bf16[512,8192]{0,1:T(8,128)(2,1)}, bf16[512,16384]{1,0:T(8,128)(2,1)}, bf16[2048,2048]{1,0:T(8,128)(2,1)}) async-done(((bf16[512,8192]{0,1:T(8,128)(2,1)}, bf16[512,16384]{1,0:T(8,128)(2,1)}, bf16[2048,2048]{1,0:T(8,128)(2,1)}), (bf16[512,8192]{0,1:T(8,128)(2,1)}, bf16[512,16384]{1,0:T(8,128)(2,1)}, bf16[2048,2048]{1,0:T(8,128)(2,1)})) %all-reduce.10.cloned.1.call-update) | async-done | bytes 33554448 | tf_op jit(solution)/shard_map/psum | solution.py:343
  (420 shorter events, 500.8 us)
Async XLA Ops:
  7.2 93.0 %all-gather.15.cloned.1.call-start = ((), (), s32[]{:S(2)}) async-start(), calls=%async_computation.5 | async-start | bytes 10485760 | tf_op jit(solution)/shard_map/all_gather | solution.py:109
  7.9 92.3 %copy-start.22 = (bf16[1,256,2048]{2,1,0:T(8,128)(2,1)S(1)}, bf16[1,256,2048]{2,1,0:T(8,128)(2,1)}, u32[]{:S(2)}) copy-start(bf16[1,256,2048]{2,1,0:T(8,128)(2,1)} %param.21) | copy-start | bytes 3145732
  7.9 181.9 %all-gather.19.cloned.1.call-start = ((), (), s32[]{:S(2)}) async-start(), calls=%async_computation.7 | async-start | bytes 10485760 | tf_op jit(solution)/shard_map/all_gather | solution.py:108
  8.7 270.7 %all-gather.23.cloned.1.call-start = ((), (), s32[]{:S(2)}) async-start(), calls=%async_computation.9 | async-start | bytes 10485760 | tf_op jit(solution)/shard_map/all_gather | solution.py:107
  9.4 97.6 %copy-start.62 = (bf16[512]{0:T(512)(128)(2,1)S(1)}, bf16[512]{0:T(512)(128)(2,1)}, u32[]{:S(2)}) copy-start(bf16[512]{0:T(512)(128)(2,1)} %param.32) | copy-start | bytes 3076
  9.4 97.6 %copy-start.63 = (bf16[512]{0:T(512)(128)(2,1)S(1)}, bf16[512]{0:T(512)(128)(2,1)}, u32[]{:S(2)}) copy-start(bf16[512]{0:T(512)(128)(2,1)} %param.33) | copy-start | bytes 3076
  9.4 97.6 %copy-start.64 = (bf16[512]{0:T(512)(128)(2,1)S(1)}, bf16[512]{0:T(512)(128)(2,1)}, u32[]{:S(2)}) copy-start(bf16[512]{0:T(512)(128)(2,1)} %param.34) | copy-start | bytes 3076
  9.4 97.6 %copy-start.65 = (bf16[512]{0:T(512)(128)(2,1)S(1)}, bf16[512]{0:T(512)(128)(2,1)}, u32[]{:S(2)}) copy-start(bf16[512]{0:T(512)(128)(2,1)} %param.35) | copy-start | bytes 3076
  9.4 354.1 %all-gather.17.cloned.1.call-start = ((), (), s32[]{:S(2)}) async-start(), calls=%async_computation.6 | async-start | bytes 9437184 | tf_op jit(solution)/shard_map/all_gather | solution.py:149
  106.9 339.7 %all-gather.21.cloned.1.call-start = ((), (), s32[]{:S(2)}) async-start(), calls=%async_computation.8 | async-start | bytes 9437184 | tf_op jit(solution)/shard_map/all_gather | solution.py:148
  137.7 151.1 %copy-start.30 = (f32[256,64]{0,1:T(8,128)}, f32[256,64]{0,1:T(8,128)S(1)}, u32[]{:S(2)}) copy-start(f32[256,64]{0,1:T(8,128)S(1)} %get-tuple-element.949) | copy-start | bytes 196612
  137.7 151.1 %copy-start.32 = (f32[256,64]{0,1:T(8,128)}, f32[256,64]{0,1:T(8,128)S(1)}, u32[]{:S(2)}) copy-start(f32[256,64]{0,1:T(8,128)S(1)} %get-tuple-element.950) | copy-start | bytes 196612
  138.4 147.4 %copy-start.40 = (f32[1,2048]{1,0:T(1,128)}, f32[1,2048]{1,0:T(1,128)S(1)}, u32[]{:S(2)}) copy-start(f32[1,2048]{1,0:T(1,128)S(1)} %get-tuple-element.947) | copy-start | bytes 24580
  202.4 340.7 %all-gather.25.cloned.1.call-start = ((), (), s32[]{:S(2)}) async-start(), calls=%async_computation.10 | async-start | bytes 10485760 | tf_op jit(solution)/shard_map/all_gather | solution.py:110
  203.0 630.2 %all-gather.27.cloned.1.call-start = ((), (), s32[]{:S(2)}) async-start(), calls=%async_computation.11 | async-start | bytes 41943040 | tf_op jit(solution)/shard_map/all_gather | solution.py:201
  203.8 928.5 %all-gather.29.cloned.1.call-start = ((), (), s32[]{:S(2)}) async-start(), calls=%async_computation.12 | async-start | bytes 41943040 | tf_op jit(solution)/shard_map/all_gather | solution.py:202
  204.5 1226.8 %all-gather.31.cloned.1.call-start = ((), (), s32[]{:S(2)}) async-start(), calls=%async_computation.13 | async-start | bytes 41943040 | tf_op jit(solution)/shard_map/all_gather | solution.py:221
  205.3 1522.3 %reduce-scatter.10.cloned.1.call-start = ((), (), s32[]{:S(2)}) async-start(), calls=%async_computation.14 | async-start | bytes 9437184 | tf_op jit(solution)/shard_map/reduce_scatter | solution.py:307
  554.1 578.2 %copy-start.20 = (bf16[256,2048]{1,0:T(8,128)(2,1)}, bf16[256,2048]{1,0:T(8,128)(2,1)S(1)}, u32[]{:S(2)}) copy-start(bf16[256,2048]{1,0:T(8,128)(2,1)S(1)} %fusion.71) | copy-start | bytes 3145732
  1637.8 180.7 %reduce-scatter.12.cloned.1.call-start = ((), (), s32[]{:S(2)}) async-start(), calls=%async_computation.15 | async-start | bytes 9437184 | tf_op jit(solution)/shard_map/reduce_scatter | solution.py:310
  1638.6 469.9 %reduce-scatter.18.cloned.1.call-start = ((), (), s32[]{:S(2)}) async-start(), calls=%async_computation.18 | async-start | bytes 41943040
  1656.2 744.3 %reduce-scatter.14.cloned.1.call-start = ((), (), s32[]{:S(2)}) async-start(), calls=%async_computation.16 | async-start | bytes 41943040 | tf_op jit(solution)/shard_map/reduce_scatter | solution.py:333
  1856.3 1105.4 %reduce-scatter.16.cloned.1.call-start = ((), (), s32[]{:S(2)}) async-start(), calls=%async_computation.17 | async-start | bytes 83886080
  1886.5 1729.6 %all-reduce.10.cloned.1.call-start = ((), (), s32[]{:S(2)}) async-start(), calls=%async_computation.19 | async-start | bytes 67108864 | tf_op jit(solution)/shard_map/psum | solution.py:343
  (71 other events, 789.3 us)
Sparse Core Ops, SparseCore 0:
  9.9 90.2 all-gather.14
  102.0 87.7 all-gather.18
  191.7 87.6 all-gather.22
  281.4 82.0 all-gather.16
  365.5 81.0 all-gather.20
  448.3 85.7 all-gather.24
  536.0 297.2 all-gather.26
  835.1 297.2 all-gather.28
  1134.1 297.2 all-gather.30
  1638.0 89.6 reduce-scatter.9
  1730.5 87.9 reduce-scatter.11
  1821.4 286.9 reduce-scatter.17
  2111.8 288.6 reduce-scatter.13
  2403.4 558.2 reduce-scatter.15
  2964.4 651.7 all-reduce.9
where the time goes:
time: 3690 us; the launch traced here: 3680 us
  waiting for transfers between devices  2980 us (81%)
  matrix products  339 us (9%)
  local copies, waits for them, and re-layouts  166 us (4%)
  other arithmetic  92.9 us (3%)
  blocking collectives  83.1 us (2%)
    unnamed x17, waiting for transfers between devices  788 us
    psum x1, waiting for transfers between devices, per_device(): lax.psum(input_share.astype(jnp.bfloat16), 'replica').astype(jnp.float32)  591 us
    reduce_scatter x1, waiting for transfers between devices, per_device(): lax.psum_scatter(jnp.concatenate([contract_rows(tokens, grad_inputs), con...  292 us
    all_gather x1, waiting for transfers between devices, per_device(): lax.all_gather(gate_weight, 'shard', axis=0, tiled=True)  279 us
    all_gather x1, waiting for transfers between devices, per_device(): lax.all_gather(up_weight, 'shard', axis=0, tiled=True)  277 us
    all_gather x1, waiting for transfers between devices, per_device(): piece = lax.all_gather(down_weight, 'shard', axis=0, tiled=True)  272 us
    all_gather x1, waiting for transfers between devices, per_device(): piece_value = lax.all_gather(value_weight, 'shard', axis=0, tiled=True)  90.7 us
    dot_general x7, matrix products, contract_cols(): lax.dot_general(left, right, (((1,), (1,)), ((), ())), preferred_element_...  77.7 us
  transfers between devices with their start and end apart: 15, of which 14 were waited for; matrix products, arithmetic and copies ran while one was open for 9% of the time, Pallas kernels for 0%

commit v1 on v0

--- a/solution.py
+++ b/solution.py
@@ -9,6 +9,18 @@
 epsilon = 1e-06
 theta_base = 500000.0
 masked_score = -1e30
+
+
+def doubled_up(x, axis, dim):
+    ways, here, turn = (lax.axis_size(axis), lax.axis_index(axis), x.shape[dim])
+    line, have = (x, 1)
+    while have < ways:
+        line = jnp.concatenate(
+            [line, lax.ppermute(line, axis, [(d, (d - have) % ways) for d in range(ways)])],
+            axis=dim,
+        )
+        have = 2 * have
+    return jnp.roll(line, here * turn, axis=dim)
 
 
 def norm_rows(values, gain):
@@ -218,7 +230,7 @@
 
     activated, act_pull = jax.vjp(activate, gate_sum, up_sum)
     activated_low = activated.astype(jnp.bfloat16)
-    piece = lax.all_gather(down_weight, "shard", axis=0, tiled=True)
+    piece = doubled_up(down_weight, "shard", 0)
     columns = activated_low
     partial_sum = jnp.dot(columns, piece, preferred_element_type=jnp.float32)
     normed_feed, feed_pull = jax.vjp(norm_rows, partial_sum, gains_wide[3])

time: 3690 us -> 4010 us (1.087)
  waiting for transfers between devices: 2980 us -> 3220 us
  local copies, waits for them, and re-layouts: 166 us -> 232 us
    ppermute x0 -> x2, waiting for transfers between devices: none -> 621 us  [doubled_up(): lax.ppermute(line, axis, [(d, (d - have) % ways) for d in range(ways)])]
    all_gather x1, waiting for transfers between devices: 279 us -> 72.4 us  [per_device(): lax.all_gather(gate_weight, 'shard', axis=0, tiled=True)]
    all_gather x1, waiting for transfers between devices: 71.9 us -> 0.01 us  [per_device(): lax.all_gather(value_low, 'replica', axis=0, tiled=True)]
    all_gather x1, waiting for transfers between devices: 70.7 us -> 0.01 us  [per_device(): lax.all_gather(key_low, 'replica', axis=0, tiled=True)]
    unnamed x149 -> x156, local copies, waits for them, and re-layouts: 49.9 us -> 94 us
  transfers between devices with their start and end apart: 15 -> 17, of which waited for: 14 -> 14; matrix products, arithmetic and copies ran while one was open for 9% -> 10% of each run, Pallas kernels for 0% -> 0%
where the time goes in v1:
time: 4010 us; the launch traced here: 4000 us
  waiting for transfers between devices  3220 us (80%)
  matrix products  337 us (8%)
  local copies, waits for them, and re-layouts  232 us (6%)
  other arithmetic  108 us (3%)
  blocking collectives  83.1 us (2%)
    unnamed x17, waiting for transfers between devices  787 us
    ppermute x2, waiting for transfers between devices, doubled_up(): lax.ppermute(line, axis, [(d, (d - have) % ways) for d in range(ways)])  621 us
    psum x1, waiting for transfers between devices, per_device(): lax.psum(input_share.astype(jnp.bfloat16), 'replica').astype(jnp.float32)  591 us
    reduce_scatter x1, waiting for transfers between devices, per_device(): lax.psum_scatter(jnp.concatenate([contract_rows(tokens, grad_inputs), con...  292 us
    all_gather x1, waiting for transfers between devices, per_device(): lax.all_gather(up_weight, 'shard', axis=0, tiled=True)  278 us
    all_gather x1, waiting for transfers between devices, per_device(): lax.all_gather(down_weight, 'shard', axis=0, tiled=True)  251 us
    unnamed x156, local copies, waits for them, and re-layouts  94 us
    all_gather x1, waiting for transfers between devices, per_device(): piece_value = lax.all_gather(value_weight, 'shard', axis=0, tiled=True)  90.7 us
  transfers between devices with their start and end apart: 17, of which 14 were waited for; matrix products, arithmetic and copies ran while one was open for 10% of the time, Pallas kernels for 0%

profile of v1, /device:TPU:0, one launch (start us, length us, event | category | flops | bytes accessed | tf_op | source)
XLA Modules:
  0.0 4001.9 jit_solution(4910728943096451063)
XLA Ops:
  9.5 90.7 %all-gather.15.cloned.1.call-done = bf16[2048,2048]{1,0:T(8,128)(2,1)} async-done(((bf16[512,2048]{1,0:T(8,128)(2,1)}), bf16[2048,2048]{1,0:T(8,128)(2,1)}) %all-gather.15.cloned.1.call-update) | async-done | bytes 8388624 | tf_op jit(solution)/shard_map/all_gather | solution.py:121
  138.4 51.5 %all-gather.19.cloned.1.call-done = bf16[2048,2048]{1,0:T(8,128)(2,1)} async-done(((bf16[512,2048]{1,0:T(8,128)(2,1)}), bf16[2048,2048]{1,0:T(8,128)(2,1)}) %all-gather.19.cloned.1.call-update) | async-done | bytes 8388624 | tf_op jit(solution)/shard_map/all_gather | solution.py:120
  206.0 199.7 %collective-permute-done = bf16[2048,2048]{1,0:T(8,128)(2,1)S(1)} collective-permute-done((bf16[2048,2048]{1,0:T(8,128)(2,1)}, bf16[2048,2048]{1,0:T(8,128)(2,1)S(1)}, u32[]{:S(2)}, u32[]{:S(2)}) %collective-permute-start) | collective-permute-done | bytes 8388640 | tf_op jit(solution)/shard_map/ppermute | solution.py:19
  448.5 48.9 %all-gather.23.cloned.1.call-done = bf16[2048,2048]{1,0:T(8,128)(2,1)} async-done(((bf16[512,2048]{1,0:T(8,128)(2,1)}), bf16[2048,2048]{1,0:T(8,128)(2,1)}) %all-gather.23.cloned.1.call-update) | async-done | bytes 8388624 | tf_op jit(solution)/shard_map/all_gather | solution.py:119
  509.6 421.0 %collective-permute-done.1 = bf16[4096,2048]{1,0:T(8,128)(2,1)} collective-permute-done((bf16[4096,2048]{1,0:T(8,128)(2,1)}, bf16[4096,2048]{1,0:T(8,128)(2,1)}, u32[]{:S(2)}, u32[]{:S(2)}) %collective-permute-start.1) | collective-permute-done | bytes 16777248 | tf_op jit(solution)/shard_map/ppermute | solution.py:19
  988.0 50.4 %while.48 = (s32[]{:T(128)}, f32[16,256]{1,0:T(8,128)S(1)}, f32[16,256]{1,0:T(8,128)S(1)}, f32[256]{0:T(256)S(1)}, bf16[2048]{0:T(1024)(128)(2,1)S(1)}, /*index=...) while((s32[]{:T(128)}, f32[16,256]{1,0:T(8,128)S(1)}, ...), condition=%wide.region_5.6_spmd.clone, body=%wide.region_2.5_spmd.clone.sunk | while | flops 552229376 | bytes 24739520 | solution.py:183
  1038.5 42.7 %while.49 = (s32[]{:T(128)}, f32[256,16,128]{0,2,1:T(8,128)}, bf16[2048,2048]{0,1:T(8,128)(2,1)}, f32[256]{0:T(256)S(1)}, bf16[2048]{0:T(1024)(128)(2,1)S(1)}, /...) while((s32[]{:T(128)}, f32[256,16,128]{0,2,1:T(8,128)}, ...), condition=%wide.region_7.8_spmd.clone, body=%wide.region_6.7_spmd.clone.sunk | while | flops 1083836928 | bytes 18120392 | solution.py:204
  1091.0 72.4 %all-gather.27.cloned.1.call-done = bf16[2048,8192]{1,0:T(8,128)(2,1)} async-done(((bf16[512,8192]{1,0:T(8,128)(2,1)}), bf16[2048,8192]{1,0:T(8,128)(2,1)}) %all-gather.27.cloned.1.call-update) | async-done | bytes 33554448 | tf_op jit(solution)/shard_map/all_gather | solution.py:213
  1163.4 21.2 fusion.95
  1184.6 277.9 %all-gather.29.cloned.1.call-done = bf16[2048,8192]{1,0:T(8,128)(2,1)} async-done(((bf16[512,8192]{1,0:T(8,128)(2,1)}), bf16[2048,8192]{1,0:T(8,128)(2,1)}) %all-gather.29.cloned.1.call-update) | async-done | bytes 33554448 | tf_op jit(solution)/shard_map/all_gather | solution.py:214
  1462.5 26.9 multiply_convert_fusion.1
  1510.5 251.0 %all-gather.31.cloned.1.call-done = bf16[8192,2048]{1,0:T(8,128)(2,1)} async-done(((bf16[2048,2048]{1,0:T(8,128)(2,1)}), bf16[8192,2048]{1,0:T(8,128)(2,1)}) %all-gather.31.cloned.1.call-update) | async-done | bytes 33554448 | tf_op jit(solution)/shard_map/all_gather | solution.py:242
  1761.6 23.3 multiply_convert_fusion
  1801.8 20.8 multiply_reduce_fusion.1
  1844.2 112.3 %while.50 = (s32[]{:T(128)}, f32[256,16,128]{0,2,1:T(8,128)}, bf16[2048,2048]{0,1:T(8,128)(2,1)}, bf16[2048,2048]{1,0:T(8,128)(2,1)}, bf16[2048,2048]{0,1:T(8,12...) while((s32[]{:T(128)}, f32[256,16,128]{0,2,1:T(8,128)}, ...), condition=%wide.region_13.14_spmd.clone, body=%wide.region_12.13_spmd.clone.sunk | while | flops 2709129728 | bytes 103219016 | solution.py:312
  1983.7 62.6 %reduce-scatter.10.cloned.1.call-done = bf16[256,2048]{0,1:T(8,128)(2,1)} async-done(((bf16[2048,2048]{0,1:T(8,128)(2,1)}), bf16[256,2048]{0,1:T(8,128)(2,1)}) %reduce-scatter.10.cloned.1.call-update) | async-done | bytes 1048592 | tf_op jit(solution)/shard_map/reduce_scatter | solution.py:319
  2062.2 75.0 %reduce-scatter.12.cloned.1.call-done = bf16[256,2048]{1,0:T(8,128)(2,1)} async-done(((bf16[2048,2048]{1,0:T(8,128)(2,1)}), bf16[256,2048]{1,0:T(8,128)(2,1)}) %reduce-scatter.12.cloned.1.call-update) | async-done | bytes 1048592 | tf_op jit(solution)/shard_map/reduce_scatter | solution.py:322
  2150.5 25.1 pad_maximum_fusion
  2176.9 29.0 convolution_convert_fusion
  2206.2 221.0 %reduce-scatter.18.cloned.1.call-done = bf16[2048,2048]{1,0:T(8,128)(2,1)} async-done(((bf16[8192,2048]{1,0:T(8,128)(2,1)}), bf16[2048,2048]{1,0:T(8,128)(2,1)}) %reduce-scatter.18.cloned.1.call-update) | async-done | bytes 8388624
  2427.1 292.0 %reduce-scatter.14.cloned.1.call-done = bf16[512,8192]{0,1:T(8,128)(2,1)} async-done(((bf16[2048,8192]{0,1:T(8,128)(2,1)}), bf16[512,8192]{0,1:T(8,128)(2,1)}) %reduce-scatter.14.cloned.1.call-update) | async-done | bytes 8388624 | tf_op jit(solution)/shard_map/reduce_scatter | solution.py:345
  2719.1 561.2 %reduce-scatter.16.cloned.1.call-done = bf16[512,16384]{1,0:T(8,128)(2,1)} async-done(((bf16[2048,16384]{1,0:T(8,128)(2,1)}), bf16[512,16384]{1,0:T(8,128)(2,1)}) %reduce-scatter.16.cloned.1.call-update) | async-done | bytes 16777232
  3284.3 41.1 %all-reduce.6 = (f32[4,2048]{1,0:T(4,128)S(1)}, f32[4]{0:T(128)S(1)}) all-reduce(f32[4,2048]{1,0:T(4,128)S(1)} %pad_maximum_fusion.3, f32[4]{0:T(128)S(1)} %pad_maximum_fusion.4), channel_id=1, replica_groups=mesh['replica'=8,'shard'=4] {'replica','shard'}, use_global_device_ids=true, to_apply=%region_28.29 | all-reduce | flops 8196 | bytes 65568 | tf_op jit(solution)/shard_map/psum | solution.py:369
  3343.7 591.2 %all-reduce.10.cloned.1.call-done = (bf16[512,8192]{0,1:T(8,128)(2,1)}, bf16[512,16384]{1,0:T(8,128)(2,1)}, bf16[2048,2048]{1,0:T(8,128)(2,1)}) async-done(((bf16[512,8192]{0,1:T(8,128)(2,1)}, bf16[512,16384]{1,0:T(8,128)(2,1)}, bf16[2048,2048]{1,0:T(8,128)(2,1)}), (bf16[512,8192]{0,1:T(8,128)(2,1)}, bf16[512,16384]{1,0:T(8,128)(2,1)}, bf16[2048,2048]{1,0:T(8,128)(2,1)})) %all-reduce.10.cloned.1.call-update) | async-done | bytes 33554448 | tf_op jit(solution)/shard_map/psum | solution.py:355
  (433 shorter events, 581.5 us)
Async XLA Ops:
  7.2 93.0 %all-gather.15.cloned.1.call-start = ((), (), s32[]{:S(2)}) async-start(), calls=%async_computation.5 | async-start | bytes 10485760 | tf_op jit(solution)/shard_map/all_gather | solution.py:121
  7.9 182.0 %all-gather.19.cloned.1.call-start = ((), (), s32[]{:S(2)}) async-start(), calls=%async_computation.7 | async-start | bytes 10485760 | tf_op jit(solution)/shard_map/all_gather | solution.py:120
  8.7 488.7 %all-gather.23.cloned.1.call-start = ((), (), s32[]{:S(2)}) async-start(), calls=%async_computation.9 | async-start | bytes 10485760 | tf_op jit(solution)/shard_map/all_gather | solution.py:119
  9.4 97.6 %copy-start.66 = (bf16[512]{0:T(512)(128)(2,1)S(1)}, bf16[512]{0:T(512)(128)(2,1)}, u32[]{:S(2)}) copy-start(bf16[512]{0:T(512)(128)(2,1)} %param.35) | copy-start | bytes 3076
  9.4 966.0 %all-gather.17.cloned.1.call-start = ((), (), s32[]{:S(2)}) async-start(), calls=%async_computation.6 | async-start | bytes 9437184 | tf_op jit(solution)/shard_map/all_gather | solution.py:161
  106.9 881.1 %all-gather.21.cloned.1.call-start = ((), (), s32[]{:S(2)}) async-start(), calls=%async_computation.8 | async-start | bytes 9437184 | tf_op jit(solution)/shard_map/all_gather | solution.py:160
  137.7 369.0 %copy-start.30 = (f32[256,64]{0,1:T(8,128)}, f32[256,64]{0,1:T(8,128)S(1)}, u32[]{:S(2)}) copy-start(f32[256,64]{0,1:T(8,128)S(1)} %get-tuple-element.949) | copy-start | bytes 196612
  137.7 369.0 %copy-start.32 = (f32[256,64]{0,1:T(8,128)}, f32[256,64]{0,1:T(8,128)S(1)}, u32[]{:S(2)}) copy-start(f32[256,64]{0,1:T(8,128)S(1)} %get-tuple-element.950) | copy-start | bytes 196612
  138.4 365.4 %copy-start.40 = (f32[1,2048]{1,0:T(1,128)}, f32[1,2048]{1,0:T(1,128)S(1)}, u32[]{:S(2)}) copy-start(f32[1,2048]{1,0:T(1,128)S(1)} %get-tuple-element.947) | copy-start | bytes 24580
  202.4 881.8 %all-gather.25.cloned.1.call-start = ((), (), s32[]{:S(2)}) async-start(), calls=%async_computation.10 | async-start | bytes 10485760 | tf_op jit(solution)/shard_map/all_gather | solution.py:122
  203.0 960.4 %all-gather.27.cloned.1.call-start = ((), (), s32[]{:S(2)}) async-start(), calls=%async_computation.11 | async-start | bytes 41943040 | tf_op jit(solution)/shard_map/all_gather | solution.py:213
  203.8 1258.7 %all-gather.29.cloned.1.call-start = ((), (), s32[]{:S(2)}) async-start(), calls=%async_computation.12 | async-start | bytes 41943040 | tf_op jit(solution)/shard_map/all_gather | solution.py:214
  204.5 1557.0 %all-gather.31.cloned.1.call-start = ((), (), s32[]{:S(2)}) async-start(), calls=%async_computation.13 | async-start | bytes 41943040 | tf_op jit(solution)/shard_map/all_gather | solution.py:242
  204.6 201.2 %collective-permute-start = (bf16[2048,2048]{1,0:T(8,128)(2,1)}, bf16[2048,2048]{1,0:T(8,128)(2,1)S(1)}, u32[]{:S(2)}, u32[]{:S(2)}) collective-permute-start(bf16[2048,2048]{1,0:T(8,128)(2,1)} %param.31), channel_id=1, source_target_pairs={{0,3},{1,0},{2,1},{3,2},{4,7},{5,4},{6,5},{7,6},{8,11},{9,8},{10,9... | collective-permute-start | bytes 25165832 | tf_op jit(solution)/shard_map/ppermute | solution.py:19
  417.8 512.9 %collective-permute-start.1 = (bf16[4096,2048]{1,0:T(8,128)(2,1)}, bf16[4096,2048]{1,0:T(8,128)(2,1)}, u32[]{:S(2)}, u32[]{:S(2)}) collective-permute-start(bf16[4096,2048]{1,0:T(8,128)(2,1)} %pad_maximum_fusion.1), channel_id=1, source_target_pairs={{0,2},{1,3},{2,0},{3,1},{4,6},{5,7},{6,4},{7,5},{8,10},{9,11},{10,... | collective-permute-start | bytes 50331656 | tf_op jit(solution)/shard_map/ppermute | solution.py:19
  419.3 1627.0 %reduce-scatter.10.cloned.1.call-start = ((), (), s32[]{:S(2)}) async-start(), calls=%async_computation.14 | async-start | bytes 9437184 | tf_op jit(solution)/shard_map/reduce_scatter | solution.py:319
  508.9 435.8 %copy-start.5 = (bf16[256,16,128]{0,2,1:T(8,128)(2,1)}, bf16[256,16,128]{0,2,1:T(8,128)(2,1)S(1)}, u32[]{:S(2)}) copy-start(bf16[256,16,128]{0,2,1:T(8,128)(2,1)S(1)} %maximum_convert_fusion) | copy-start | bytes 3145732
  1091.0 371.5 %copy-start.17 = (bf16[256,2048]{1,0:T(8,128)(2,1)}, bf16[256,2048]{1,0:T(8,128)(2,1)S(1)}, u32[]{:S(2)}) copy-start(bf16[256,2048]{1,0:T(8,128)(2,1)S(1)} %fusion.73) | copy-start | bytes 3145732
  1510.5 274.4 %copy-start.54 = (f32[256]{0:T(256)}, f32[256]{0:T(256)S(1)}, u32[]{:S(2)}) copy-start(f32[256]{0:T(256)S(1)} %multiply_multiply_fusion.8) | copy-start | bytes 3076
  1956.5 180.7 %reduce-scatter.12.cloned.1.call-start = ((), (), s32[]{:S(2)}) async-start(), calls=%async_computation.15 | async-start | bytes 9437184 | tf_op jit(solution)/shard_map/reduce_scatter | solution.py:322
  1957.3 469.9 %reduce-scatter.18.cloned.1.call-start = ((), (), s32[]{:S(2)}) async-start(), calls=%async_computation.18 | async-start | bytes 41943040
  1974.8 744.4 %reduce-scatter.14.cloned.1.call-start = ((), (), s32[]{:S(2)}) async-start(), calls=%async_computation.16 | async-start | bytes 41943040 | tf_op jit(solution)/shard_map/reduce_scatter | solution.py:345
  2175.7 1104.7 %reduce-scatter.16.cloned.1.call-start = ((), (), s32[]{:S(2)}) async-start(), calls=%async_computation.17 | async-start | bytes 83886080
  2206.0 1728.9 %all-reduce.10.cloned.1.call-start = ((), (), s32[]{:S(2)}) async-start(), calls=%async_computation.19 | async-start | bytes 67108864 | tf_op jit(solution)/shard_map/psum | solution.py:355
  (74 other events, 1270.6 us)
Sparse Core Ops, SparseCore 0:
  9.9 90.2 all-gather.14
  102.1 87.7 all-gather.18
  191.7 305.6 all-gather.22
  499.4 82.0 all-gather.16
  583.5 81.0 all-gather.20
  666.3 153.4 all-gather.24
  821.6 341.7 all-gather.26
  1165.2 297.2 all-gather.28
  1464.3 297.2 all-gather.30
  1956.7 89.5 reduce-scatter.9
  2049.2 87.9 reduce-scatter.11
  2140.1 286.9 reduce-scatter.17
  2430.5 288.5 reduce-scatter.13
  2722.0 558.2 reduce-scatter.15
  3283.1 651.7 all-reduce.9
